TPU v7x, 32 devices: a whole 2x2x4 slice. The times are simulated.
32 devices in a mesh: row: 8 (over z, y), col: 4 (over x, core).
Axes of the slice: x: 2, y: 2, z: 4, core: 2. Of those that a mesh axis runs over, the one named last changes fastest.
Arguments:
- trailing: bfloat16 [12288, 12288], P('row', 'col'), may hold values from -6 to 6
- rows_a: int32 [8, 12], replicated, may hold values from 0 to 11, as said below
- counts_a: int32 [8], replicated, may hold values from 1 to 12, as said below
- factor_a: bfloat16 [12288, 512], P('row'), may hold values from -0.0546875 to 0.0546875
- rows_b: int32 [8, 12], replicated, may hold values from 0 to 11, as said below
- counts_b: int32 [8], replicated, may hold values from 1 to 12, as said below
- factor_b: bfloat16 [12288, 512], P('row'), may hold values from -0.0546875 to 0.0546875
- factor_top: bfloat16 [512, 512], replicated, may hold values from -0.25 to 0.25
- base_a: float32 [512, 512], P('col'), may hold values from -3 to 3
- base_b: float32 [512, 512], P('col'), may hold values from -3 to 3
Outputs:
- column_a: bfloat16 [12288, 512], P('row')
- diag_a: float32 [512, 512], P('col')
- column_b: bfloat16 [12288, 512], P('row')
- top_b: bfloat16 [512, 512], P('col')
- diag_b: float32 [512, 512], P('col')
Inputs may be any that keep to these rules, and one draw needn't show every extreme that they name: `rows_a`: the first counts_a[r] entries of row r are distinct; the rest of the row is padding. `counts_a`: some owner uses all 12 slots in every draw. `rows_b`: the first counts_b[r] entries of row r are distinct and lie among the first counts_a[r] entries of row r of rows_a; the rest is padding. counts_b[r] <= counts_a[r]; some owner uses all 12 slots in every draw.
All inputs are finite; a program needn't handle non-finite values.
Results may differ from a plain program's by a relative error of at most 0.007.
Values may be sent and summed in bfloat16 or wider, within the bound.
A program may use at most 128 MiB of HBM per device.

v0:
```python
import jax
import jax.numpy as jnp
from jax import lax
from jax.sharding import PartitionSpec as P

BS = 128
W = 512
RBD = 12
PAD = 12


def spread_2(value, axis, source):
    kept = jnp.where(lax.axis_index(axis) == source, value, 0).astype(value.dtype)
    return lax.psum(kept, axis)


def contract_rows(former, latter):
    return lax.dot_general(
        former, latter, (((0,), (0,)), ((), ())), preferred_element_type=jnp.float32
    )


def slot_live(counts, owner_idx):
    live_count = lax.dynamic_index_in_dim(counts, owner_idx, 0, keepdims=False)
    return jnp.arange(PAD, dtype=jnp.int32) < live_count


def on_device(
    trailing, rows_a, counts_a, factor_a, rows_b, counts_b, factor_b, factor_top, base_a, base_b
):
    row_count = lax.axis_size("row")
    col_count = lax.axis_size("col")
    fanout = row_count // col_count
    row_index = lax.axis_index("row")
    col_index = lax.axis_index("col")
    col_blocks = trailing.shape[1] // BS
    part_width = W // col_count
    slot_rows = PAD * BS
    share_rows = slot_rows // col_count
    width_start = col_index * part_width
    share_start = col_index * share_rows
    slab_blocks = trailing.reshape(RBD, BS, trailing.shape[1])

    def row_gate(live_rows):
        return jnp.repeat(live_rows.astype(jnp.float32), BS)[:, None]

    def partial_product(rows, counts, factor):
        own_rows = lax.dynamic_index_in_dim(rows, row_index, 0, keepdims=False)
        row_slab = jnp.take(slab_blocks, own_rows, axis=0).reshape(slot_rows, trailing.shape[1])
        pieces = []
        targets = []
        flags = []
        for offset in range(fanout):
            source = col_index + offset * col_count
            pieces.append(spread_2(factor, "row", source))
            src_rows = lax.dynamic_index_in_dim(rows, source, 0, keepdims=False)
            targets.append(src_rows * fanout + offset)
            flags.append(slot_live(counts, source))
        received = jnp.stack(pieces).reshape(fanout * PAD, BS * W)
        target = jnp.concatenate(targets)
        live_src = jnp.concatenate(flags)
        selector = (
            (jnp.arange(col_blocks, dtype=jnp.int32)[:, None] == target[None, :])
            & live_src[None, :]
        ).astype(jnp.bfloat16)
        spread = jnp.dot(selector, received, preferred_element_type=jnp.float32).astype(
            jnp.bfloat16
        )
        return jnp.dot(
            row_slab, spread.reshape(col_blocks * BS, W), preferred_element_type=jnp.float32
        )

    def finish(partial_value, live_rows, addend):
        gate = row_gate(live_rows)
        reduced = lax.psum_scatter(partial_value, "col", scatter_dimension=0, tiled=True)
        if addend is not None:
            reduced = reduced + addend(share_start, share_rows)
        share_gate = lax.dynamic_slice_in_dim(gate, share_start, share_rows, 0)
        share_out = (-reduced * share_gate).astype(jnp.bfloat16)
        return lax.all_gather(share_out, "col", axis=0, tiled=True)

    def row_sums(pieces_in):
        return lax.psum(pieces_in, "row")

    live_a = slot_live(counts_a, row_index)
    live_b = slot_live(counts_b, row_index)
    column_a = finish(partial_product(rows_a, counts_a, factor_a), live_a, None)
    own_rows_a = lax.dynamic_index_in_dim(rows_a, row_index, 0, keepdims=False)
    own_rows_b = lax.dynamic_index_in_dim(rows_b, row_index, 0, keepdims=False)
    pairing = (
        (own_rows_b[:, None] == own_rows_a[None, :]) & live_a[None, :] & live_b[:, None]
    ).astype(jnp.bfloat16)
    carried = (
        jnp.dot(pairing, column_a.reshape(PAD, BS * W), preferred_element_type=jnp.float32)
        .astype(jnp.bfloat16)
        .reshape(slot_rows, W)
    )
    width_a = lax.dynamic_slice_in_dim(column_a, width_start, part_width, 1)
    width_c = lax.dynamic_slice_in_dim(carried, width_start, part_width, 1)
    sums_a = row_sums((contract_rows(width_a, factor_a), contract_rows(width_c, factor_b)))
    diag_a = base_a - sums_a[0]
    top_b = (
        -(
            sums_a[1]
            + jnp.dot(diag_a, factor_top.astype(jnp.float32), precision=lax.Precision.HIGHEST)
        )
    ).astype(jnp.bfloat16)

    def cross_rows(first_row, row_total):
        picked = lax.dynamic_slice_in_dim(carried, first_row, row_total, 0)
        return jnp.dot(picked, factor_top, preferred_element_type=jnp.float32)

    column_b = finish(partial_product(rows_b, counts_b, factor_b), live_b, cross_rows)
    width_b = lax.dynamic_slice_in_dim(column_b, width_start, part_width, 1)
    sums_b = row_sums((contract_rows(width_b, factor_b),))
    top_whole = lax.all_gather(top_b, "col", axis=0, tiled=True)
    top_cols = lax.dynamic_slice_in_dim(top_whole, width_start, part_width, 1)
    diag_b = base_b - sums_b[0] - contract_rows(top_cols, factor_top)
    return (column_a, diag_a, column_b, top_b, diag_b)


def solution(mesh):
    in_specs = (
        P("row", "col"),
        P(),
        P(),
        P("row", None),
        P(),
        P(),
        P("row", None),
        P(),
        P("col", None),
        P("col", None),
    )
    out_specs = (P("row", None), P("col", None), P("row", None), P("col", None), P("col", None))
    return jax.shard_map(
        on_device, mesh=mesh, in_specs=in_specs, out_specs=out_specs, check_vma=False
    )
```

profile of v0, /device:TPU:0, one launch (start us, length us, event | category | flops | bytes accessed | tf_op | source)
XLA Modules:
  0.0 484.4 jit_solution(11630658327107411684)
XLA Ops:
  7.2 4.8 select_bitcast_fusion.1
  13.5 9.4 %gather_fusion = bf16[12,128,3072]{2,1,0:T(8,128)(2,1)} fusion(bf16[12,128,3072]{2,1,0:T(8,128)(2,1)} %bitcast.59, s32[1024]{0:T(1024)S(1)} %pad_clamp_fusion.1), kind=kCustom, calls=%fused_computation.clone | custom fusion | bytes 18874416 | tf_op jit(solution)/shard_map/jit(_take)/gather | solution.py:49
  26.7 8.4 %broadcast_select_fusion.1 = bf16[12,128,3072]{2,1,0:T(8,128)(2,1)} fusion(bf16[12,128,3072]{2,1,0:T(8,128)(2,1)} %gather_fusion, pred[12]{0:T(512)(128)(4,1)S(1)} %get-tuple-element.15), kind=kLoop, calls=%fused_computation.6 | loop fusion | flops 4718592 | bytes 18874380 | tf_op jit(solution)/shard_map/jit(_take)/select_n | solution.py:49
  35.0 191.1 %all-reduce.7.cloned.1.call-done = (bf16[1,1536,512]{2,1,0:T(8,128)(2,1)}, bf16[1,1536,512]{2,1,0:T(8,128)(2,1)}, bf16[1,1536,512]{2,1,0:T(8,128)(2,1)}, bf16[1,1536,512]{2,1,0:T(8,128)(2,1)}) async-done(((bf16[1,1536,512]{2,1,0:T(8,128)(2,1)}, bf16[1,1536,512]{2,1,0:T(8,128)(2,1)}, bf16[1,1536,512]{2,1,0:T(8,128)(2,1)}, bf16[1,1536,512]{2,1,0:T(8,128)(2,1)}), (bf16[1,1536,512]{2,1,0:T(8,128)(2,1)}, ...) | async-done | bytes 6291472 | tf_op jit(solution)/shard_map/psum | solution.py:14
  226.1 3.8 pad_maximum_fusion
  229.9 5.2 %reshape.70 = bf16[24,65536]{1,0:T(8,128)(2,1)} reshape(bf16[2,1536,512]{2,1,0:T(8,128)(2,1)} %pad_maximum_fusion) | data formatting | bytes 6291456 | tf_op jit(solution)/shard_map/reshape | solution.py:59
  235.1 4.5 convolution_convert_fusion.1
  239.6 5.2 %reshape.71 = bf16[3072,512]{1,0:T(8,128)(2,1)} reshape(bf16[24,65536]{1,0:T(8,128)(2,1)} %convolution_convert_fusion.1) | data formatting | bytes 6291456 | tf_op jit(solution)/shard_map/reshape | solution.py:70
  244.8 10.6 %fusion.53 = f32[1536,512]{1,0:T(8,128)} fusion(bf16[1536,3072]{1,0:T(8,128)(2,1)} %bitcast.62, bf16[3072,512]{1,0:T(8,128)(2,1)} %reshape.71), kind=kOutput, calls=%fused_computation.96 | convolution fusion | flops 4831838208 | bytes 15728640 | tf_op jit(solution)/shard_map/dot_general | solution.py:69
  255.5 9.7 %gather_fusion.1 = bf16[12,128,3072]{2,1,0:T(8,128)(2,1)} fusion(bf16[12,128,3072]{2,1,0:T(8,128)(2,1)} %bitcast.60, s32[1024]{0:T(1024)S(1)} %pad_clamp_fusion), kind=kCustom, calls=%fused_computation.1.clone | custom fusion | bytes 18874416 | tf_op jit(solution)/shard_map/jit(_take)/gather | solution.py:49
  267.3 8.4 %broadcast_select_fusion = bf16[12,128,3072]{2,1,0:T(8,128)(2,1)} fusion(bf16[12,128,3072]{2,1,0:T(8,128)(2,1)} %gather_fusion.1, pred[12]{0:T(512)(128)(4,1)S(1)} %get-tuple-element.13), kind=kLoop, calls=%fused_computation.5 | loop fusion | flops 4718592 | bytes 18874380 | tf_op jit(solution)/shard_map/jit(_take)/select_n | solution.py:49
  275.7 16.8 %reduce-scatter.3.cloned.1.call-done = f32[384,512]{1,0:T(8,128)} async-done(((f32[1536,512]{1,0:T(8,128)}), f32[384,512]{1,0:T(8,128)}) %reduce-scatter.3.cloned.1.call-update) | async-done | bytes 786448 | tf_op jit(solution)/shard_map/reduce_scatter | solution.py:75
  292.5 2.0 multiply_convert_fusion
  294.8 3.4 pad_maximum_fusion.1
  298.1 5.2 %reshape.73 = bf16[24,65536]{1,0:T(8,128)(2,1)} reshape(bf16[2,1536,512]{2,1,0:T(8,128)(2,1)} %pad_maximum_fusion.1) | data formatting | bytes 6291456 | tf_op jit(solution)/shard_map/reshape | solution.py:59
  303.3 4.5 convolution_convert_fusion
  307.8 5.2 %reshape.74 = bf16[3072,512]{1,0:T(8,128)(2,1)} reshape(bf16[24,65536]{1,0:T(8,128)(2,1)} %convolution_convert_fusion) | data formatting | bytes 6291456 | tf_op jit(solution)/shard_map/reshape | solution.py:70
  313.0 10.6 %fusion.54 = f32[1536,512]{1,0:T(8,128)} fusion(bf16[1536,3072]{1,0:T(8,128)(2,1)} %bitcast.61, bf16[3072,512]{1,0:T(8,128)(2,1)} %reshape.74), kind=kOutput, calls=%fused_computation.97 | convolution fusion | flops 4831838208 | bytes 15728640 | tf_op jit(solution)/shard_map/dot_general | solution.py:69
  325.8 2.2 reshape.75
  328.0 2.1 convolution_convert_fusion.2
  330.1 3.6 reshape.76
  333.7 28.1 %reduce-scatter.5.cloned.1.call-done = f32[384,512]{1,0:T(8,128)} async-done(((f32[1536,512]{1,0:T(8,128)}), f32[384,512]{1,0:T(8,128)}) %reduce-scatter.5.cloned.1.call-update) | async-done | bytes 786448 | tf_op jit(solution)/shard_map/reduce_scatter | solution.py:75
  361.7 2.4 fusion.2
  364.2 2.1 fusion.7
  366.3 2.7 fusion.10
  369.0 14.9 %all-gather.5.cloned.1.call-done = bf16[1536,512]{1,0:T(8,128)(2,1)} async-done(((bf16[384,512]{1,0:T(8,128)(2,1)}), bf16[1536,512]{1,0:T(8,128)(2,1)}) %all-gather.5.cloned.1.call-update) | async-done | bytes 1572880 | tf_op jit(solution)/shard_map/all_gather | solution.py:80
  383.9 2.1 fusion.5
  386.1 77.7 %all-reduce.5.cloned.1.call-done = (f32[128,512]{1,0:T(8,128)}, f32[128,512]{1,0:T(8,128)}, f32[128,512]{1,0:T(8,128)}) async-done(((f32[128,512]{1,0:T(8,128)}, f32[128,512]{1,0:T(8,128)}, f32[128,512]{1,0:T(8,128)}), (f32[128,512]{1,0:T(8,128)}, f32[128,512]{1,0:T(8,128)}, f32[128,512]{1,0:T(8,128)})) %all-reduce.5.cloned.1.call-update) | async-done | bytes 786448 | tf_op jit(solution)/shard_map/psum | solution.py:83
  464.8 1.4 fusion.4
  466.2 7.2 %all_gather.11 = bf16[512,512]{1,0:T(8,128)(2,1)S(1)} all-gather(bf16[128,512]{1,0:T(8,128)(2,1)S(1)} %fusion.4), channel_id=1, replica_groups=mesh['row'=8,'col'=4] {'col'}, dimensions={0}, use_global_device_ids=true | all-gather | bytes 655360 | tf_op jit(solution)/shard_map/all_gather | solution.py:116
  473.4 1.9 convolution_subtract_fusion
  476.4 1.1 copy.31
  (62 shorter events, 12.0 us)
Async XLA Ops:
  7.2 354.6 %copy-start = (bf16[512,512]{1,0:T(8,128)(2,1)S(1)}, bf16[512,512]{1,0:T(8,128)(2,1)}, u32[]{:S(2)}) copy-start(bf16[512,512]{1,0:T(8,128)(2,1)} %param.19) | copy-start | bytes 1572868
  7.2 218.9 %all-reduce.7.cloned.1.call-start = ((), (), s32[]{:S(2)}) async-start(), calls=%async_computation.7 | async-start | bytes 12582912 | tf_op jit(solution)/shard_map/psum | solution.py:14
  12.0 280.4 %reduce-scatter.3.cloned.1.call-start = ((), (), s32[]{:S(2)}) async-start(), calls=%async_computation.2 | async-start | bytes 3932160 | tf_op jit(solution)/shard_map/reduce_scatter | solution.py:75
  13.5 9.5 %copy-start.9 = (s32[8]{0:T(128)S(1)}, s32[8]{0:T(128)}, u32[]{:S(2)}) copy-start(s32[8]{0:T(128)} %param.17) | copy-start | bytes 100
  13.5 9.4 %copy-start.10 = (s32[8]{0:T(128)S(1)}, s32[8]{0:T(128)}, u32[]{:S(2)}) copy-start(s32[8]{0:T(128)} %param.14) | copy-start | bytes 100
  255.4 70.3 %all-gather.3.cloned.1.call-start = ((), (), s32[]{:S(2)}) async-start(), calls=%async_computation.3 | async-start | bytes 1966080 | tf_op jit(solution)/shard_map/all_gather | solution.py:80
  267.3 27.5 %copy-start.4 = (bf16[1,1536,512]{2,1,0:T(8,128)(2,1)S(1)}, bf16[1,1536,512]{2,1,0:T(8,128)(2,1)}, u32[]{:S(2)}) copy-start(bf16[1,1536,512]{2,1,0:T(8,128)(2,1)} %get-tuple-element.11) | copy-start | bytes 4718596
  294.5 67.2 %reduce-scatter.5.cloned.1.call-start = ((), (), s32[]{:S(2)}) async-start(), calls=%async_computation.4 | async-start | bytes 3932160 | tf_op jit(solution)/shard_map/reduce_scatter | solution.py:75
  323.6 60.3 %all-gather.5.cloned.1.call-start = ((), (), s32[]{:S(2)}) async-start(), calls=%async_computation.5 | async-start | bytes 1966080 | tf_op jit(solution)/shard_map/all_gather | solution.py:80
  330.1 34.1 %copy-start.1 = (bf16[1536,512]{1,0:T(8,128)(2,1)S(1)}, bf16[1536,512]{1,0:T(8,128)(2,1)}, u32[]{:S(2)}) copy-start(bf16[1536,512]{1,0:T(8,128)(2,1)} %param.18) | copy-start | bytes 4718596
  364.1 99.6 %all-reduce.5.cloned.1.call-start = ((), (), s32[]{:S(2)}) async-start(), calls=%async_computation.6 | async-start | bytes 1572864 | tf_op jit(solution)/shard_map/psum | solution.py:83
  366.3 97.4 %copy-start.7 = (f32[128,512]{1,0:T(8,128)S(1)}, f32[128,512]{1,0:T(8,128)}, u32[]{:S(2)}) copy-start(f32[128,512]{1,0:T(8,128)} %param.20) | copy-start | bytes 786436
  369.0 104.4 %copy-start.8 = (f32[128,512]{1,0:T(8,128)S(1)}, f32[128,512]{1,0:T(8,128)}, u32[]{:S(2)}) copy-start(f32[128,512]{1,0:T(8,128)} %param.21) | copy-start | bytes 786436
  386.0 89.3 %copy-start.2 = (bf16[1536,512]{1,0:T(8,128)(2,1)S(1)}, bf16[1536,512]{1,0:T(8,128)(2,1)}, u32[]{:S(2)}) copy-start(bf16[1536,512]{1,0:T(8,128)(2,1)} %all-gather.3.cloned.1.call-done) | copy-start | bytes 4718596
  464.7 11.7 %copy-start.5 = (f32[128,512]{1,0:T(8,128)}, f32[128,512]{1,0:T(8,128)S(1)}, u32[]{:S(2)}) copy-start(f32[128,512]{1,0:T(8,128)S(1)} %sub.9) | copy-start | bytes 786436
  464.7 11.7 %copy-start.3 = (bf16[1536,512]{1,0:T(8,128)(2,1)S(1)}, bf16[1536,512]{1,0:T(8,128)(2,1)}, u32[]{:S(2)}) copy-start(bf16[1536,512]{1,0:T(8,128)(2,1)} %all-gather.5.cloned.1.call-done) | copy-start | bytes 4718596
  466.2 11.4 %copy-start.6 = (bf16[128,512]{1,0:T(8,128)(2,1)}, bf16[128,512]{1,0:T(8,128)(2,1)S(1)}, u32[]{:S(2)}) copy-start(bf16[128,512]{1,0:T(8,128)(2,1)S(1)} %fusion.4) | copy-start | bytes 393220
Sparse Core Ops, SparseCore 0:
  13.0 213.0 all-reduce.6
  255.5 36.8 reduce-scatter.2
  294.6 19.6 all-gather.2
  323.8 37.9 reduce-scatter.4
  364.3 19.6 all-gather.4
  388.1 75.5 all-reduce.4
where the time goes:
time: 486 us; the launch traced here: 484 us
  waiting for transfers between devices  329 us (68%)
  local copies, waits for them, and re-layouts  48.8 us (10%)
  matrix products  45 us (9%)
  other arithmetic  40.1 us (8%)
  between operations  14.3 us (3%)
  blocking collectives  7.15 us (1%)
    psum x1, waiting for transfers between devices, spread_2(): return lax.psum(kept, axis)  191 us
    psum x1, waiting for transfers between devices, row_sums(): return lax.psum(pieces_in, 'row')  77.7 us
    reduce_scatter x2, waiting for transfers between devices, finish(): lax.psum_scatter(partial_value, 'col', scatter_dimension=0, tiled=True)  44.8 us
    dot_general x2, matrix products, partial_product(): jnp.dot(row_slab, spread.reshape(col_blocks * BS, W), preferred_element_t...  21.2 us
    gather x2, local copies, waits for them, and re-layouts, partial_product(): jnp.take(slab_blocks, own_rows, axis=0)  19.1 us
    select_n x3, other arithmetic, partial_product(): jnp.take(slab_blocks, own_rows, axis=0)  16.8 us
    all_gather x2, waiting for transfers between devices, finish(): return lax.all_gather(share_out, 'col', axis=0, tiled=True)  14.9 us
    another operation x3, other arithmetic, partial_product(): received = jnp.stack(pieces).reshape(fanout * PAD, BS * W)  11.9 us
  transfers between devices with their start and end apart: 6, of which 5 were waited for; matrix products, arithmetic and copies ran while one was open for 18% of the time, Pallas kernels for 0%

commit v1 on v0

v1 whole, which is shorter than its diff:
```python
import functools

import jax
import jax.numpy as jnp
from jax import lax
from jax.experimental import pallas as pl
from jax.experimental.pallas import tpu as pltpu
from jax.sharding import PartitionSpec as P

MESH = pl.DeviceIdType.MESH
CHUNK_SLOTS = 2


def spread_multiply_kernel(
    nz, ny, col_count, fanout, slots, block,
    idx_ref, fa_ref, fb_ref, slab_ref, out_ref,
    held, slab, acc, recv_sem, send_sem, local_sem, slab_sem,
):
    row = lax.axis_index("row")
    col = lax.axis_index("col")
    z = row // ny
    y = row % ny
    chunk = CHUNK_SLOTS * block
    steps = slots // CHUNK_SLOTS
    rows, width = acc.shape[1:]

    def slab_copy(j):
        return pltpu.make_async_copy(
            slab_ref.at[:, pl.ds(pl.multiple_of(j * block, block), block)],
            slab.at[j],
            slab_sem.at[j],
        )

    @pl.loop(0, slab.shape[0])
    def _(j):
        slab_copy(j).start()

    neighbours = (
        (z < nz - 1, row + ny),
        (z > 0, row - ny),
        (y < ny - 1, row + 1),
        (y > 0, row - 1),
    )
    barrier = pltpu.get_barrier_semaphore()
    for there, who in neighbours:
        @pl.when(there)
        def _():
            pl.semaphore_signal(barrier, inc=1, device_id={"row": who}, device_id_type=MESH)
    greeted = (
        jnp.minimum(nz - 1 - z, 1)
        + jnp.minimum(z, 1)
        + jnp.minimum(ny - 1 - y, 1)
        + jnp.minimum(y, 1)
    )
    pl.semaphore_wait(barrier, greeted)

    sources, sends = [], []
    for part in range(fanout):
        owner = col + part * col_count
        oz, oy = owner // ny, owner % ny
        line = y == oy
        sources.append(row == owner)
        sends.append(
            (
                line & (z >= oz) & (z < nz - 1),
                line & (z <= oz) & (z > 0),
                (y >= oy) & (y < ny - 1),
                (y <= oy) & (y > 0),
            )
        )

    for part in range(fanout):
        @pl.when(sources[part])
        def _():
            for node, factor in enumerate((fa_ref, fb_ref)):
                pltpu.make_async_copy(
                    factor, held.at[node, part], local_sem.at[node * fanout + part]
                ).start()
            for node, factor in enumerate((fa_ref, fb_ref)):
                pltpu.make_async_copy(
                    factor, held.at[node, part], local_sem.at[node * fanout + part]
                ).wait()

    def hop(step, part, way):
        node, at = step // steps, step % steps
        piece = held.at[node, part, pl.ds(pl.multiple_of(at * chunk, chunk), chunk)]
        return pltpu.make_async_remote_copy(
            src_ref=piece,
            dst_ref=piece,
            send_sem=send_sem.at[step, part, way],
            recv_sem=recv_sem.at[step, part],
            device_id={"row": neighbours[way][1]},
            device_id_type=MESH,
        )

    acc[...] = jnp.zeros_like(acc)
    tile = 256

    @pl.loop(0, slab.shape[0])
    def _(j):
        slab_copy(j).wait()

    @pl.loop(0, 2 * steps)
    def _(step):
        for part in range(fanout):
            @pl.when(jnp.logical_not(sources[part]))
            def _():
                hop(step, part, 0).wait_recv()
            for way in range(4):
                @pl.when(sends[part][way])
                def _():
                    hop(step, part, way).start()
        node, at = step // steps, step % steps

        @pl.loop(0, rows // tile)
        def _(r):
            here = pl.ds(pl.multiple_of(r * tile, tile), tile)
            total = acc[node, here, :]
            for part in range(fanout):
                left = jnp.concatenate(
                    [
                        slab[idx_ref[node, part, at * CHUNK_SLOTS + k], here, :]
                        for k in range(CHUNK_SLOTS)
                    ],
                    axis=1,
                )
                right = held[node, part, pl.ds(pl.multiple_of(at * chunk, chunk), chunk), :]
                total += jnp.dot(left, right, preferred_element_type=jnp.float32)
            acc[node, here, :] = total

            @pl.when(at == steps - 1)
            def _():
                out_ref[node, here, :] = total.astype(out_ref.dtype)

    @pl.loop(0, 2 * steps)
    def _(step):
        for part in range(fanout):
            for way in range(4):
                @pl.when(sends[part][way])
                def _():
                    hop(step, part, way).wait_send()


def spread_multiply(idx, factor_a, factor_b, trailing, row_count, col_count):
    slots = idx.shape[2]
    rows, width = factor_a.shape
    block = rows // slots
    fanout = row_count // col_count
    ny = max(col_count // 2, 1)
    nz = row_count // ny
    steps = slots // CHUNK_SLOTS
    return pl.pallas_call(
        functools.partial(
            spread_multiply_kernel, nz, ny, col_count, fanout, slots, block
        ),
        out_shape=jax.ShapeDtypeStruct((2, trailing.shape[0], width), jnp.bfloat16),
        in_specs=[
            pl.BlockSpec(memory_space=pltpu.SMEM),
            pl.BlockSpec(memory_space=pl.ANY),
            pl.BlockSpec(memory_space=pl.ANY),
            pl.BlockSpec(memory_space=pl.ANY),
        ],
        out_specs=pl.BlockSpec(memory_space=pltpu.VMEM),
        scratch_shapes=[
            pltpu.VMEM((2, fanout, rows, width), jnp.bfloat16),
            pltpu.VMEM((trailing.shape[1] // block, trailing.shape[0], block), jnp.bfloat16),
            pltpu.VMEM((2, trailing.shape[0], width), jnp.float32),
            pltpu.SemaphoreType.DMA((2 * steps, fanout)),
            pltpu.SemaphoreType.DMA((2 * steps, fanout, 4)),
            pltpu.SemaphoreType.DMA((2 * fanout,)),
            pltpu.SemaphoreType.DMA((trailing.shape[1] // block,)),
        ],
        compiler_params=pltpu.CompilerParams(
            collective_id=0, has_side_effects=True, vmem_limit_bytes=60 * 1024 * 1024
        ),
        name="spread_multiply",
    )(idx, factor_a, factor_b, trailing)


def contract_rows(former, latter):
    return lax.dot_general(
        former, latter, (((0,), (0,)), ((), ())), preferred_element_type=jnp.float32
    )


def on_device(
    trailing, rows_a, counts_a, factor_a, rows_b, counts_b, factor_b, factor_top, base_a, base_b
):
    row_count = lax.axis_size("row")
    col_count = lax.axis_size("col")
    fanout = row_count // col_count
    row_index = lax.axis_index("row")
    col_index = lax.axis_index("col")
    slots = rows_a.shape[1]
    total_rows, width = factor_a.shape
    block = total_rows // slots
    row_blocks = trailing.shape[0] // block
    part_width = width // col_count
    width_start = col_index * part_width
    slot_ids = jnp.arange(slots, dtype=jnp.int32)

    def own(table):
        return lax.dynamic_index_in_dim(table, row_index, 0, keepdims=False)

    live_a = slot_ids < own(counts_a)
    live_b = slot_ids < own(counts_b)
    own_a, own_b = own(rows_a), own(rows_b)
    blocks = jnp.arange(row_blocks, dtype=jnp.int32)
    gate_a = jnp.any((own_a[None, :] == blocks[:, None]) & live_a[None, :], axis=1)
    gate_b = jnp.any((own_b[None, :] == blocks[:, None]) & live_b[None, :], axis=1)

    def masked(factor, live):
        return jnp.where(
            live[:, None, None], factor.reshape(slots, block, width), 0
        ).reshape(total_rows, width).astype(factor.dtype)

    parts = jnp.arange(fanout, dtype=jnp.int32)
    owners = col_index + parts * col_count
    idx = jnp.stack(
        [jnp.take(rows, owners, axis=0) * fanout + parts[:, None] for rows in (rows_a, rows_b)]
    ).astype(jnp.int32)
    part = spread_multiply(
        idx, masked(factor_a, live_a), masked(factor_b, live_b), trailing, row_count, col_count
    )
    reduced = lax.psum_scatter(part, "col", scatter_dimension=2, tiled=True).astype(jnp.float32)

    def gated(value, gate):
        return jnp.where(
            gate[:, None, None], value.reshape(row_blocks, block, -1), 0
        ).reshape(row_blocks * block, -1)

    def by_slot(value, own_rows, live):
        picked = jnp.take(value.reshape(row_blocks, block, -1), own_rows, axis=0)
        return jnp.where(live[:, None, None], picked, 0).reshape(total_rows, -1)

    col_a = gated(-reduced[0], gate_a).astype(jnp.bfloat16)
    whole_a = lax.all_gather(col_a, "col", axis=1, tiled=True)
    column_a = by_slot(whole_a, own_a, live_a)
    top_part = lax.dynamic_slice_in_dim(factor_top, width_start, part_width, 1)
    cross = jnp.dot(whole_a, top_part, preferred_element_type=jnp.float32)
    col_b = gated(-(reduced[1] + cross), gate_b).astype(jnp.bfloat16)
    column_b = by_slot(
        lax.all_gather(col_b, "col", axis=1, tiled=True), own_b, live_b
    )
    sums = lax.psum(
        (
            contract_rows(by_slot(col_a, own_a, live_a), factor_a),
            contract_rows(by_slot(col_a, own_b, live_b), factor_b),
            contract_rows(by_slot(col_b, own_b, live_b), factor_b),
        ),
        "row",
    )
    diag_a = base_a - sums[0]
    top_b = (
        -(
            sums[1]
            + jnp.dot(diag_a, factor_top.astype(jnp.float32), precision=lax.Precision.HIGHEST)
        )
    ).astype(jnp.bfloat16)
    top_whole = lax.all_gather(top_b, "col", axis=0, tiled=True)
    top_cols = lax.dynamic_slice_in_dim(top_whole, width_start, part_width, 1)
    diag_b = base_b - sums[2] - contract_rows(top_cols, factor_top)
    return (column_a, diag_a, column_b, top_b, diag_b)


def solution(mesh):
    in_specs = (
        P("row", "col"),
        P(),
        P(),
        P("row", None),
        P(),
        P(),
        P("row", None),
        P(),
        P("col", None),
        P("col", None),
    )
    out_specs = (P("row", None), P("col", None), P("row", None), P("col", None), P("col", None))
    return jax.shard_map(
        on_device, mesh=mesh, in_specs=in_specs, out_specs=out_specs, check_vma=False
    )
```

time: 486 us -> 507 us (1.043)
  Pallas kernels: 0 us -> 291 us
  waiting for transfers between devices: 329 us -> 144 us
  matrix products: 45 us -> 9.1 us
  other arithmetic: 40.1 us -> 11.9 us
  local copies, waits for them, and re-layouts: 48.8 us -> 28.6 us
    pallas_call x0 -> x1, Pallas kernels: none -> 291 us  [spread_multiply(): pl.pallas_call(functools.partial(spread_multiply_kernel, nz, ny, col_coun...]
    psum x2 -> x1, waiting for transfers between devices: 269 us -> 71.7 us  [on_device(): lax.psum((contract_rows(by_slot(col_a, own_a, live_a), factor_a), contrac...]
    unnamed x6 -> x5, waiting for transfers between devices: 0.1 us -> 46.2 us
    reduce_scatter x2 -> x0, waiting for transfers between devices: 44.8 us -> none  [finish(): lax.psum_scatter(partial_value, 'col', scatter_dimension=0, tiled=True)]
    dot_general x6 -> x1, matrix products: 34.7 us -> 1.99 us  [on_device(): cross = jnp.dot(whole_a, top_part, preferred_element_type=jnp.float32)]
    reshape x6 -> x0, local copies, waits for them, and re-layouts: 26.5 us -> none  [the longest x2 10.4 us: partial_product(): received = jnp.stack(pieces).reshape(fanout * PAD, BS * W)]
    unnamed x28 -> x20, local copies, waits for them, and re-layouts: 2.5 us -> 17.3 us
    another operation x3 -> x2, other arithmetic: 11.9 us -> 0.66 us  [on_device(): jnp.stack([jnp.take(rows, owners, axis=0) * fanout + parts[:, None] for r...]
  transfers between devices with their start and end apart: 6 -> 4, of which waited for: 5 -> 4; matrix products, arithmetic and copies ran while one was open for 18% -> 2% of each run, Pallas kernels for 0% -> 0%
where the time goes in v1:
time: 507 us; the launch traced here: 506 us
  Pallas kernels  291 us (57%)
  waiting for transfers between devices  144 us (28%)
  local copies, waits for them, and re-layouts  28.6 us (6%)
  between operations  14 us (3%)
  other arithmetic  11.9 us (2%)
  matrix products  9.1 us (2%)
  blocking collectives  7.15 us (1%)
    pallas_call x1, Pallas kernels, spread_multiply(): pl.pallas_call(functools.partial(spread_multiply_kernel, nz, ny, col_coun...  291 us
    psum x1, waiting for transfers between devices, on_device(): lax.psum((contract_rows(by_slot(col_a, own_a, live_a), factor_a), contrac...  71.7 us
    unnamed x5, waiting for transfers between devices  46.2 us
    unnamed x20, local copies, waits for them, and re-layouts  17.3 us
    all_gather x1, waiting for transfers between devices, on_device(): whole_a = lax.all_gather(col_a, 'col', axis=1, tiled=True)  15.5 us
    all_gather x1, waiting for transfers between devices, on_device(): lax.all_gather(col_b, 'col', axis=1, tiled=True)  10.4 us
  transfers between devices with their start and end apart: 4, of which 4 were waited for; matrix products, arithmetic and copies ran while one was open for 2% of the time, Pallas kernels for 0%

profile of v1, /device:TPU:0, one launch (start us, length us, event | category | flops | bytes accessed | tf_op | source)
XLA Modules:
  0.0 505.9 jit_solution(12426732919968800451)
XLA Ops:
  7.3 1.3 dynamic_slice.22
  8.6 0.6 iota_compare_fusion.2
  9.3 1.2 dynamic_slice.20
  10.5 0.6 iota_compare_fusion.3
  11.3 1.2 gather_fusion
  12.5 1.2 gather_fusion.1
  14.4 3.5 broadcast_select_fusion
  17.9 291.2 %spread_multiply.1 = bf16[2,1536,512]{2,1,0:T(8,128)(2,1)} custom-call(s32[2,2,12]{2,1,0:T(2,128)} %pad_add_fusion.idx_ref, bf16[1536,512]{1,0:T(8,128)(2,1)} %get-tuple-element.22.fa_ref, bf16[1536,512]{1,0:T(8,128)(2,1)} %get-tuple-element.21.fb_ref, bf16[1536,3072]{1,0:T(8,128)(2,1)} %slab_ref.1), custom_call_target="tpu_custom_call" | custom-call | tf_op jit(solution)/shard_map/spread_multiply/pallas_call | solution.py:152
  309.1 8.8 %copy.15 = bf16[2,1536,512]{1,0,2:T(2,128)(2,1)} copy(bf16[2,1536,512]{2,1,0:T(8,128)(2,1)} %spread_multiply.1) | data formatting | bytes 6291456
  317.9 4.3 copy.17
  322.3 0.7 compare_and_fusion
  323.2 45.7 %reduce-scatter.4.cloned.1.call-done = bf16[128,3072]{1,0:T(8,128)(2,1)} async-done(((bf16[512,3072]{1,0:T(8,128)(2,1)}), bf16[128,3072]{1,0:T(8,128)(2,1)}) %reduce-scatter.4.cloned.1.call-update) | async-done | bytes 786448
  368.9 2.6 reshape.177
  371.5 0.8 copy.16
  372.4 1.0 fusion.5
  373.9 0.6 gather_fusion.5
  375.3 2.5 fusion.22
  377.8 15.5 %all-gather.3.cloned.1.call-done = bf16[1536,512]{1,0:T(8,128)(2,1)} async-done(((bf16[1536,128]{1,0:T(8,128)(2,1)}), bf16[1536,512]{1,0:T(8,128)(2,1)}) %all-gather.3.cloned.1.call-update) | async-done | bytes 1572880 | tf_op jit(solution)/shard_map/all_gather | solution.py:237
  393.4 2.0 fusion.2
  396.2 0.7 copy-done.1
  396.9 1.1 fusion.23
  398.0 1.1 fusion.24
  399.8 2.1 gather_fusion.2
  401.8 1.4 select_select_fusion.1
  403.2 71.7 %all-reduce.3.cloned.1.call-done = (f32[128,512]{1,0:T(8,128)}, f32[128,512]{1,0:T(8,128)}, f32[128,512]{1,0:T(8,128)}) async-done(((f32[128,512]{1,0:T(8,128)}, f32[128,512]{1,0:T(8,128)}, f32[128,512]{1,0:T(8,128)}), (f32[128,512]{1,0:T(8,128)}, f32[128,512]{1,0:T(8,128)}, f32[128,512]{1,0:T(8,128)})) %all-reduce.3.cloned.1.call-update) | async-done | bytes 786448 | tf_op jit(solution)/shard_map/psum | solution.py:245
  475.0 1.0 sub.9
  476.0 1.4 fusion.4
  477.4 7.1 %all_gather.11 = bf16[512,512]{1,0:T(8,128)(2,1)S(1)} all-gather(bf16[128,512]{1,0:T(8,128)(2,1)S(1)} %fusion.4), channel_id=1, replica_groups=mesh['row'=8,'col'=4] {'col'}, dimensions={0}, use_global_device_ids=true | all-gather | bytes 655360 | tf_op jit(solution)/shard_map/all_gather | solution.py:260
  484.6 1.0 convolution_subtract_fusion
  485.6 10.4 %all-gather.5.cloned.1.call-done = bf16[1536,512]{1,0:T(8,128)(2,1)} async-done(((bf16[1536,128]{1,0:T(8,128)(2,1)}), bf16[1536,512]{1,0:T(8,128)(2,1)}) %all-gather.5.cloned.1.call-update) | async-done | bytes 1572880 | tf_op jit(solution)/shard_map/all_gather | solution.py:243
  495.9 2.1 gather_fusion.4
  498.0 1.4 select_select_fusion
  (45 shorter events, 3.9 us)
Async XLA Ops:
  7.2 386.2 %copy-start = (bf16[512,512]{1,0:T(8,128)(2,1)S(1)}, bf16[512,512]{1,0:T(8,128)(2,1)}, u32[]{:S(2)}) copy-start(bf16[512,512]{1,0:T(8,128)(2,1)} %param.23) | copy-start | bytes 1572868
  7.2 361.7 %reduce-scatter.4.cloned.1.call-start = ((), (), s32[]{:S(2)}) async-start(), calls=%async_computation.3 | async-start | bytes 3932160
  322.3 71.1 %all-gather.3.cloned.1.call-start = ((), (), s32[]{:S(2)}) async-start(), calls=%async_computation.1 | async-start | bytes 1966080 | tf_op jit(solution)/shard_map/all_gather | solution.py:237
  373.4 101.5 %all-reduce.3.cloned.1.call-start = ((), (), s32[]{:S(2)}) async-start(), calls=%async_computation.4 | async-start | bytes 1572864 | tf_op jit(solution)/shard_map/psum | solution.py:245
  395.4 2.7 copy-start.2
  395.4 1.6 copy-start.1
  399.2 96.8 %all-gather.5.cloned.1.call-start = ((), (), s32[]{:S(2)}) async-start(), calls=%async_computation.2 | async-start | bytes 1966080 | tf_op jit(solution)/shard_map/all_gather | solution.py:243
  401.8 73.2 %copy-start.5 = (f32[128,512]{1,0:T(8,128)S(1)}, f32[128,512]{1,0:T(8,128)}, u32[]{:S(2)}) copy-start(f32[128,512]{1,0:T(8,128)} %param.24) | copy-start | bytes 786436
  403.2 81.4 %copy-start.6 = (f32[128,512]{1,0:T(8,128)S(1)}, f32[128,512]{1,0:T(8,128)}, u32[]{:S(2)}) copy-start(f32[128,512]{1,0:T(8,128)} %param.25) | copy-start | bytes 786436
  475.0 9.6 %copy-start.7 = (f32[128,512]{1,0:T(8,128)S(1)}, f32[128,512]{1,0:T(8,128)}, u32[]{:S(2)}) copy-start(f32[128,512]{1,0:T(8,128)} %get-tuple-element.10) | copy-start | bytes 786436
  476.0 9.6 %copy-start.3 = (f32[128,512]{1,0:T(8,128)}, f32[128,512]{1,0:T(8,128)S(1)}, u32[]{:S(2)}) copy-start(f32[128,512]{1,0:T(8,128)S(1)} %sub.9) | copy-start | bytes 786436
  477.4 20.6 %copy-start.4 = (bf16[128,512]{1,0:T(8,128)(2,1)}, bf16[128,512]{1,0:T(8,128)(2,1)S(1)}, u32[]{:S(2)}) copy-start(bf16[128,512]{1,0:T(8,128)(2,1)S(1)} %fusion.4) | copy-start | bytes 393220
Sparse Core Ops, SparseCore 0:
  322.4 46.4 reduce-scatter.3
  373.5 19.7 all-gather.2
  399.3 75.6 all-reduce.2
  476.9 18.9 all-gather.4

commit v2 on v0

v2 whole, which is shorter than its diff:
```python
import jax
import jax.numpy as jnp
from jax import lax
from jax.sharding import PartitionSpec as P


def contract_rows(former, latter):
    return lax.dot_general(
        former, latter, (((0,), (0,)), ((), ())), preferred_element_type=jnp.float32
    )


def on_device(
    trailing, rows_a, counts_a, factor_a, rows_b, counts_b, factor_b, factor_top, base_a, base_b
):
    row_count = lax.axis_size("row")
    col_count = lax.axis_size("col")
    fanout = row_count // col_count
    row_index = lax.axis_index("row")
    col_index = lax.axis_index("col")
    slots = rows_a.shape[1]
    total_rows, width = factor_a.shape
    block = total_rows // slots
    row_blocks = trailing.shape[0] // block
    part_width = width // col_count
    width_start = col_index * part_width
    slot_ids = jnp.arange(slots, dtype=jnp.int32)

    def own(table):
        return lax.dynamic_index_in_dim(table, row_index, 0, keepdims=False)

    live_a = slot_ids < own(counts_a)
    live_b = slot_ids < own(counts_b)
    own_a, own_b = own(rows_a), own(rows_b)
    blocks = jnp.arange(row_blocks, dtype=jnp.int32)
    gate_a = jnp.any((own_a[None, :] == blocks[:, None]) & live_a[None, :], axis=1)
    gate_b = jnp.any((own_b[None, :] == blocks[:, None]) & live_b[None, :], axis=1)

    pieces = jnp.stack([factor_a, factor_b]).reshape(
        2, row_count, total_rows // row_count, width
    )
    arrived = []
    for shift in range(row_count):
        piece = lax.dynamic_index_in_dim(
            pieces, (row_index + shift) % row_count, 1, keepdims=False
        )
        if shift:
            pairs = [
                (
                    owner * col_count + owner % col_count,
                    (owner + shift) % row_count * col_count + owner % col_count,
                )
                for owner in range(row_count)
            ]
            piece = lax.ppermute(piece, ("row", "col"), pairs)
        arrived.append(piece)
    arrived = jnp.stack(arrived)
    mine = jnp.stack(
        [
            lax.dynamic_index_in_dim(
                arrived,
                (row_index - col_index - part * col_count) % row_count,
                0,
                keepdims=False,
            )
            for part in range(fanout)
        ],
        axis=1,
    )
    held = lax.all_gather(mine, "row", axis=2, tiled=True)
    owners = col_index + jnp.arange(fanout, dtype=jnp.int32) * col_count

    def partial_product(node, rows, counts):
        own_rows = jnp.take(rows, owners, axis=0)
        live = slot_ids[None, :] < jnp.take(counts, owners, axis=0)[:, None]
        match = (own_rows[None, :, :] == blocks[:, None, None]) & live[None, :, :]
        filled = jnp.any(match, axis=2).reshape(-1)
        source = jnp.argmax(match, axis=2).astype(jnp.int32)
        source = (source + jnp.arange(fanout, dtype=jnp.int32) * slots).reshape(-1)
        picked = jnp.take(held[node].reshape(fanout * slots, block, width), source, axis=0)
        spread = jnp.where(filled[:, None, None], picked, 0).reshape(-1, width)
        return jnp.dot(trailing, spread, preferred_element_type=jnp.float32).astype(
            jnp.bfloat16
        )

    part = jnp.stack(
        [partial_product(0, rows_a, counts_a), partial_product(1, rows_b, counts_b)]
    )
    reduced = lax.psum_scatter(part, "col", scatter_dimension=2, tiled=True).astype(jnp.float32)

    def gated(value, gate):
        return jnp.where(
            gate[:, None, None], value.reshape(row_blocks, block, -1), 0
        ).reshape(row_blocks * block, -1)

    def by_slot(value, own_rows, live):
        picked = jnp.take(value.reshape(row_blocks, block, -1), own_rows, axis=0)
        return jnp.where(live[:, None, None], picked, 0).reshape(total_rows, -1)

    col_a = gated(-reduced[0], gate_a).astype(jnp.bfloat16)
    whole_a = lax.all_gather(col_a, "col", axis=1, tiled=True)
    column_a = by_slot(whole_a, own_a, live_a)
    top_part = lax.dynamic_slice_in_dim(factor_top, width_start, part_width, 1)
    cross = jnp.dot(whole_a, top_part, preferred_element_type=jnp.float32)
    col_b = gated(-(reduced[1] + cross), gate_b).astype(jnp.bfloat16)
    column_b = by_slot(
        lax.all_gather(col_b, "col", axis=1, tiled=True), own_b, live_b
    )
    sums = lax.psum(
        (
            contract_rows(by_slot(col_a, own_a, live_a), factor_a),
            contract_rows(by_slot(col_a, own_b, live_b), factor_b),
            contract_rows(by_slot(col_b, own_b, live_b), factor_b),
        ),
        "row",
    )
    diag_a = base_a - sums[0]
    top_b = (
        -(
            sums[1]
            + jnp.dot(diag_a, factor_top.astype(jnp.float32), precision=lax.Precision.HIGHEST)
        )
    ).astype(jnp.bfloat16)
    top_whole = lax.all_gather(top_b, "col", axis=0, tiled=True)
    top_cols = lax.dynamic_slice_in_dim(top_whole, width_start, part_width, 1)
    diag_b = base_b - sums[2] - contract_rows(top_cols, factor_top)
    return (column_a, diag_a, column_b, top_b, diag_b)


def solution(mesh):
    in_specs = (
        P("row", "col"),
        P(),
        P(),
        P("row", None),
        P(),
        P(),
        P("row", None),
        P(),
        P("col", None),
        P("col", None),
    )
    out_specs = (P("row", None), P("col", None), P("row", None), P("col", None), P("col", None))
    return jax.shard_map(
        on_device, mesh=mesh, in_specs=in_specs, out_specs=out_specs, check_vma=False
    )
```

time: 486 us -> 360 us (0.74)
  waiting for transfers between devices: 329 us -> 227 us
  starting transfers between devices: 0.43 us -> 19.3 us
  matrix products: 45 us -> 27.1 us
  other arithmetic: 40.1 us -> 26.2 us
  local copies, waits for them, and re-layouts: 48.8 us -> 37.5 us
    psum x2 -> x1, waiting for transfers between devices: 269 us -> 69.1 us  [on_device(): lax.psum((contract_rows(by_slot(col_a, own_a, live_a), factor_a), contrac...]
    all_gather x2 -> x3, waiting for transfers between devices: 14.9 us -> 117 us  [the longest x1 95.2 us: on_device(): held = lax.all_gather(mine, 'row', axis=2, tiled=True)]
    reshape x6 -> x2, local copies, waits for them, and re-layouts: 26.5 us -> 0.16 us  [partial_product(): source = (source + jnp.arange(fanout, dtype=jnp.int32) * slots).reshape(-1)]
    ppermute x0 -> x7, starting transfers between devices: none -> 18.9 us  [on_device(): piece = lax.ppermute(piece, ('row', 'col'), pairs)]
    dot_general x6 -> x3, matrix products: 34.7 us -> 19 us  [the longest x2 17 us: partial_product(): jnp.dot(trailing, spread, preferred_element_type=jnp.float32)]
    reduce_scatter x2 -> x1, waiting for transfers between devices: 44.8 us -> 34.1 us  [on_device(): lax.psum_scatter(part, 'col', scatter_dimension=2, tiled=True)]
    select_n x3 -> x13, other arithmetic: 16.8 us -> 8.78 us  [the longest x2 4.6 us: partial_product(): spread = jnp.where(filled[:, None, None], picked, 0).reshape(-1, width)]
    another operation x3 -> x4, other arithmetic: 11.9 us -> 5.02 us  [the longest x2 2.16 us: partial_product(): source = jnp.argmax(match, axis=2).astype(jnp.int32)]
  transfers between devices with their start and end apart: 6 -> 12, of which waited for: 5 -> 7; matrix products, arithmetic and copies ran while one was open for 18% -> 9% of each run, Pallas kernels for 0% -> 0%
where the time goes in v2:
time: 360 us; the launch traced here: 359 us
  waiting for transfers between devices  227 us (63%)
  local copies, waits for them, and re-layouts  37.5 us (10%)
  matrix products  27.1 us (8%)
  other arithmetic  26.2 us (7%)
  starting transfers between devices  19.3 us (5%)
  between operations  14.4 us (4%)
  blocking collectives  7.15 us (2%)
    all_gather x1, waiting for transfers between devices, on_device(): held = lax.all_gather(mine, 'row', axis=2, tiled=True)  95.2 us
    psum x1, waiting for transfers between devices, on_device(): lax.psum((contract_rows(by_slot(col_a, own_a, live_a), factor_a), contrac...  69.1 us
    reduce_scatter x1, waiting for transfers between devices, on_device(): lax.psum_scatter(part, 'col', scatter_dimension=2, tiled=True)  34.1 us
    ppermute x7, starting transfers between devices, on_device(): piece = lax.ppermute(piece, ('row', 'col'), pairs)  18.9 us
    dot_general x2, matrix products, partial_product(): jnp.dot(trailing, spread, preferred_element_type=jnp.float32)  17 us
    all_gather x1, waiting for transfers between devices, on_device(): whole_a = lax.all_gather(col_a, 'col', axis=1, tiled=True)  13.2 us
    gather x2, local copies, waits for them, and re-layouts, partial_product(): jnp.take(held[node].reshape(fanout * slots, block, width), source, axis=0)  8.76 us
    all_gather x1, waiting for transfers between devices, on_device(): lax.all_gather(col_b, 'col', axis=1, tiled=True)  8.72 us
  transfers between devices with their start and end apart: 12, of which 7 were waited for; matrix products, arithmetic and copies ran while one was open for 9% of the time, Pallas kernels for 0%

profile of v2, /device:TPU:0, one launch (start us, length us, event | category | flops | bytes accessed | tf_op | source)
XLA Modules:
  0.0 359.1 jit_solution(10162166294966140)
XLA Ops:
  7.3 2.9 fusion.22
  10.2 5.7 %collective-permute-start = (bf16[2,192,512]{2,1,0:T(8,128)(2,1)}, bf16[2,192,512]{2,1,0:T(8,128)(2,1)}, u32[]{:S(2)}, u32[]{:S(2)}) collective-permute-start(bf16[2,192,512]{2,1,0:T(8,128)(2,1)} %get-tuple-element.26), channel_id=1, source_target_pairs={{0,4},{5,9},{10,14},{15,19},{16,20},{21,25},{26,30},{31,3}} | collective-permute-start | bytes 1179656 | tf_op jit(solution)/shard_map/ppermute | solution.py:55
  15.9 2.1 collective-permute-start.1
  18.0 2.0 collective-permute-start.2
  20.0 4.5 %collective-permute-start.3 = (bf16[2,192,512]{2,1,0:T(8,128)(2,1)S(1)}, bf16[2,192,512]{2,1,0:T(8,128)(2,1)}, u32[]{:S(2)}, u32[]{:S(2)}) collective-permute-start(bf16[2,192,512]{2,1,0:T(8,128)(2,1)S(1)} %get-tuple-element.29), channel_id=1, source_target_pairs={{0,16},{5,21},{10,26},{15,31},{16,0},{21,5},{26,10},{31,15}} | collective-permute-start | bytes 1179656 | tf_op jit(solution)/shard_map/ppermute | solution.py:55
  24.5 2.1 collective-permute-start.4
  26.6 1.7 bitcast_dynamic-update-slice_fusion.7
  37.3 2.3 collective-permute-done.5
  39.6 4.2 %collective-permute-done.6 = bf16[2,192,512]{2,1,0:T(8,128)(2,1)S(1)} collective-permute-done((bf16[2,192,512]{2,1,0:T(8,128)(2,1)S(1)}, bf16[2,192,512]{2,1,0:T(8,128)(2,1)S(1)}, u32[]{:S(2)}, u32[]{:S(2)}) %collective-permute-start.6) | collective-permute-done | bytes 393248 | tf_op jit(solution)/shard_map/ppermute | solution.py:55
  50.7 95.2 %all-gather.4.cloned.1.call-done = bf16[2,2,1536,512]{3,2,0,1:T(8,128)(2,1)} async-done(((bf16[2,2,192,512]{3,2,0,1:T(8,128)(2,1)}), bf16[2,2,1536,512]{3,2,0,1:T(8,128)(2,1)}) %all-gather.4.cloned.1.call-update) | async-done | bytes 6291472 | tf_op jit(solution)/shard_map/all_gather | solution.py:70
  145.9 5.9 %fusion.37 = (bf16[1,2,1536,512]{3,2,0,1:T(8,128)(2,1)}, bf16[1,2,1536,512]{3,2,0,1:T(8,128)(2,1)}) fusion(bf16[2,2,1536,512]{3,2,0,1:T(8,128)(2,1)} %all-gather.4.cloned.1.call-done), kind=kLoop, calls=%fused_computation.126 | loop fusion | bytes 12582912 | tf_op jit(solution)/shard_map/slice | solution.py:80
  151.8 4.4 %gather_fusion.2 = bf16[24,128,512]{2,1,0:T(8,128)(2,1)} fusion(bf16[24,128,512]{2,1,0:T(8,128)(2,1)} %bitcast.98, s32[1024]{0:T(1024)S(1)} %pad_clamp_fusion.3), kind=kCustom, calls=%fused_computation.2.clone | custom fusion | bytes 6291552 | tf_op jit(solution)/shard_map/jit(_take)/gather | solution.py:80
  156.2 2.3 select_select_fusion.1
  158.5 9.0 %fusion = bf16[1,1536,512]{1,2,0:T(8,128)(2,1)} fusion(bf16[3072,512]{1,0:T(8,128)(2,1)S(1)} %bitcast.101, bf16[1536,3072]{1,0:T(8,128)(2,1)} %param.20), kind=kOutput, calls=%fused_computation.32 | convolution fusion | flops 4832624640 | bytes 14155776 | tf_op jit(solution)/shard_map/dot_general | solution.py:82
  167.5 4.4 %gather_fusion.5 = bf16[24,128,512]{2,1,0:T(8,128)(2,1)} fusion(bf16[24,128,512]{2,1,0:T(8,128)(2,1)} %bitcast.97, s32[1024]{0:T(1024)S(1)} %pad_clamp_fusion.2), kind=kCustom, calls=%fused_computation.7.clone | custom fusion | bytes 6291552 | tf_op jit(solution)/shard_map/jit(_take)/gather | solution.py:80
  171.9 2.3 select_select_fusion
  174.2 8.0 %fusion.1 = bf16[1,1536,512]{1,2,0:T(8,128)(2,1)S(1)} fusion(bf16[3072,512]{1,0:T(8,128)(2,1)S(1)} %bitcast.102, bf16[1536,3072]{1,0:T(8,128)(2,1)} %param.20), kind=kOutput, calls=%fused_computation.33 | convolution fusion | flops 4832624640 | bytes 14155776 | tf_op jit(solution)/shard_map/dot_general | solution.py:82
  182.2 1.9 pad_maximum_fusion
  186.2 34.1 %reduce-scatter.2.cloned.1.call-done = bf16[2,1536,128]{1,2,0:T(8,128)(2,1)} async-done(((bf16[2,1536,512]{1,2,0:T(8,128)(2,1)}), bf16[2,1536,128]{1,2,0:T(8,128)(2,1)}) %reduce-scatter.2.cloned.1.call-update) | async-done | bytes 786448 | tf_op jit(solution)/shard_map/reduce_scatter | solution.py:89
  227.7 2.5 fusion.38
  230.2 13.2 %all-gather.6.cloned.1.call-done = bf16[1536,512]{0,1:T(8,128)(2,1)} async-done(((bf16[1536,128]{0,1:T(8,128)(2,1)}), bf16[1536,512]{0,1:T(8,128)(2,1)}) %all-gather.6.cloned.1.call-update) | async-done | bytes 1572880 | tf_op jit(solution)/shard_map/all_gather | solution.py:101
  243.4 2.0 fusion.4
  251.1 2.6 copy.27
  253.7 2.1 gather_fusion.6
  257.2 69.1 %all-reduce.3.cloned.1.call-done = (f32[128,512]{1,0:T(8,128)}, f32[128,512]{1,0:T(8,128)}, f32[128,512]{1,0:T(8,128)}) async-done(((f32[128,512]{1,0:T(8,128)}, f32[128,512]{1,0:T(8,128)}, f32[128,512]{1,0:T(8,128)}), (f32[128,512]{1,0:T(8,128)}, f32[128,512]{1,0:T(8,128)}, f32[128,512]{1,0:T(8,128)})) %all-reduce.3.cloned.1.call-update) | async-done | bytes 786448 | tf_op jit(solution)/shard_map/psum | solution.py:109
  327.3 1.4 fusion.6
  328.7 7.1 %all_gather.15 = bf16[512,512]{1,0:T(8,128)(2,1)S(1)} all-gather(bf16[128,512]{1,0:T(8,128)(2,1)S(1)} %fusion.6), channel_id=1, replica_groups=mesh['row'=8,'col'=4] {'col'}, dimensions={0}, use_global_device_ids=true | all-gather | bytes 655360 | tf_op jit(solution)/shard_map/all_gather | solution.py:124
  335.9 1.9 convolution_subtract_fusion
  337.8 8.7 %all-gather.8.cloned.1.call-done = bf16[1536,512]{0,1:T(8,128)(2,1)} async-done(((bf16[1536,128]{0,1:T(8,128)(2,1)}), bf16[1536,512]{0,1:T(8,128)(2,1)}) %all-gather.8.cloned.1.call-update) | async-done | bytes 1572880 | tf_op jit(solution)/shard_map/all_gather | solution.py:107
  346.5 2.6 copy.30
  349.1 2.1 gather_fusion.8
  351.2 1.4 select_select_fusion.2
  (108 shorter events, 33.1 us)
Async XLA Ops:
  7.2 236.2 %copy-start = (bf16[512,512]{1,0:T(8,128)(2,1)S(1)}, bf16[512,512]{1,0:T(8,128)(2,1)}, u32[]{:S(2)}) copy-start(bf16[512,512]{1,0:T(8,128)(2,1)} %param.27) | copy-start | bytes 1572868
  7.2 19.4 %copy-start.3 = (bf16[1536,512]{1,0:T(8,128)(2,1)S(1)}, bf16[1536,512]{1,0:T(8,128)(2,1)}, u32[]{:S(2)}) copy-start(bf16[1536,512]{1,0:T(8,128)(2,1)} %param.26) | copy-start | bytes 4718596
  7.2 138.7 %all-gather.4.cloned.1.call-start = ((), (), s32[]{:S(2)}) async-start(), calls=%async_computation.1 | async-start | bytes 7077888 | tf_op jit(solution)/shard_map/all_gather | solution.py:70
  10.2 19.1 %collective-permute-start = (bf16[2,192,512]{2,1,0:T(8,128)(2,1)}, bf16[2,192,512]{2,1,0:T(8,128)(2,1)}, u32[]{:S(2)}, u32[]{:S(2)}) collective-permute-start(bf16[2,192,512]{2,1,0:T(8,128)(2,1)} %get-tuple-element.26), channel_id=1, source_target_pairs={{0,4},{5,9},{10,14},{15,19},{16,20},{21,25},{26,30},{31,3}} | collective-permute-start | bytes 1179656 | tf_op jit(solution)/shard_map/ppermute | solution.py:55
  15.9 15.8 %collective-permute-start.1 = (bf16[2,192,512]{2,1,0:T(8,128)(2,1)}, bf16[2,192,512]{2,1,0:T(8,128)(2,1)}, u32[]{:S(2)}, u32[]{:S(2)}) collective-permute-start(bf16[2,192,512]{2,1,0:T(8,128)(2,1)} %get-tuple-element.27), channel_id=1, source_target_pairs={{0,8},{5,13},{10,18},{15,23},{16,24},{21,29},{26,2},{31,7}} | collective-permute-start | bytes 1179656 | tf_op jit(solution)/shard_map/ppermute | solution.py:55
  18.0 16.1 %collective-permute-start.2 = (bf16[2,192,512]{2,1,0:T(8,128)(2,1)}, bf16[2,192,512]{2,1,0:T(8,128)(2,1)}, u32[]{:S(2)}, u32[]{:S(2)}) collective-permute-start(bf16[2,192,512]{2,1,0:T(8,128)(2,1)} %get-tuple-element.28), channel_id=1, source_target_pairs={{0,12},{5,17},{10,22},{15,27},{16,28},{21,1},{26,6},{31,11}} | collective-permute-start | bytes 1179656 | tf_op jit(solution)/shard_map/ppermute | solution.py:55
  20.0 15.1 %collective-permute-start.3 = (bf16[2,192,512]{2,1,0:T(8,128)(2,1)S(1)}, bf16[2,192,512]{2,1,0:T(8,128)(2,1)}, u32[]{:S(2)}, u32[]{:S(2)}) collective-permute-start(bf16[2,192,512]{2,1,0:T(8,128)(2,1)S(1)} %get-tuple-element.29), channel_id=1, source_target_pairs={{0,16},{5,21},{10,26},{15,31},{16,0},{21,5},{26,10},{31,15}} | collective-permute-start | bytes 1179656 | tf_op jit(solution)/shard_map/ppermute | solution.py:55
  24.5 11.7 %collective-permute-start.4 = (bf16[2,192,512]{2,1,0:T(8,128)(2,1)S(1)}, bf16[2,192,512]{2,1,0:T(8,128)(2,1)}, u32[]{:S(2)}, u32[]{:S(2)}) collective-permute-start(bf16[2,192,512]{2,1,0:T(8,128)(2,1)S(1)} %get-tuple-element.30), channel_id=1, source_target_pairs={{0,20},{5,25},{10,30},{15,3},{16,4},{21,9},{26,14},{31,19}} | collective-permute-start | bytes 1179656 | tf_op jit(solution)/shard_map/ppermute | solution.py:55
  28.2 2.5 copy-start.9
  29.4 10.2 %collective-permute-start.5 = (bf16[2,192,512]{2,1,0:T(8,128)(2,1)S(1)}, bf16[2,192,512]{2,1,0:T(8,128)(2,1)S(1)}, u32[]{:S(2)}, u32[]{:S(2)}) collective-permute-start(bf16[2,192,512]{2,1,0:T(8,128)(2,1)S(1)} %fusion.16), channel_id=1, source_target_pairs={{0,24},{5,29},{10,2},{15,7},{16,8},{21,13},{26,18},{31,23}} | collective-permute-start | bytes 1179656 | tf_op jit(solution)/shard_map/ppermute | solution.py:55
  31.7 12.0 %collective-permute-start.6 = (bf16[2,192,512]{2,1,0:T(8,128)(2,1)S(1)}, bf16[2,192,512]{2,1,0:T(8,128)(2,1)S(1)}, u32[]{:S(2)}, u32[]{:S(2)}) collective-permute-start(bf16[2,192,512]{2,1,0:T(8,128)(2,1)S(1)} %get-tuple-element.25), channel_id=1, source_target_pairs={{0,28},{5,1},{10,6},{15,11},{16,12},{21,17},{26,22},{31,27}} | collective-permute-start | bytes 1179656 | tf_op jit(solution)/shard_map/ppermute | solution.py:55
  36.2 8.7 %copy-start.12 = (s32[8,12]{1,0:T(8,128)S(1)}, s32[8,12]{1,0:T(8,128)}, u32[]{:S(2)}) copy-start(s32[8,12]{1,0:T(8,128)} %param.21) | copy-start | bytes 1156
  36.2 9.3 %copy-start.13 = (s32[8,12]{1,0:T(8,128)S(1)}, s32[8,12]{1,0:T(8,128)}, u32[]{:S(2)}) copy-start(s32[8,12]{1,0:T(8,128)} %param.24) | copy-start | bytes 1156
  36.2 9.8 %copy-start.1 = (s32[8]{0:T(128)S(1)}, s32[8]{0:T(128)}, u32[]{:S(2)}) copy-start(s32[8]{0:T(128)} %param.22) | copy-start | bytes 100
  37.2 9.4 %copy-start.2 = (s32[8]{0:T(128)S(1)}, s32[8]{0:T(128)}, u32[]{:S(2)}) copy-start(s32[8]{0:T(128)} %param.25) | copy-start | bytes 100
  44.8 175.5 %reduce-scatter.2.cloned.1.call-start = ((), (), s32[]{:S(2)}) async-start(), calls=%async_computation.2 | async-start | bytes 3932160 | tf_op jit(solution)/shard_map/reduce_scatter | solution.py:89
  174.2 8.0 %copy-start.6 = (bf16[1,1536,512]{1,2,0:T(8,128)(2,1)S(1)}, bf16[1,1536,512]{1,2,0:T(8,128)(2,1)}, u32[]{:S(2)}) copy-start(bf16[1,1536,512]{1,2,0:T(8,128)(2,1)} %fusion) | copy-start | bytes 4718596
  184.1 59.3 %all-gather.6.cloned.1.call-start = ((), (), s32[]{:S(2)}) async-start(), calls=%async_computation.3 | async-start | bytes 1966080 | tf_op jit(solution)/shard_map/all_gather | solution.py:101
  221.6 1.1 copy-start.4
  223.6 102.7 %all-reduce.3.cloned.1.call-start = ((), (), s32[]{:S(2)}) async-start(), calls=%async_computation.5 | async-start | bytes 1572864 | tf_op jit(solution)/shard_map/psum | solution.py:109
  245.5 5.0 %copy-start.5 = (bf16[1536,128]{0,1:T(8,128)(2,1)}, bf16[1536,128]{0,1:T(8,128)(2,1)S(1)}, u32[]{:S(2)}) copy-start(bf16[1536,128]{0,1:T(8,128)(2,1)S(1)} %fusion.4) | copy-start | bytes 1179652
  250.5 96.0 %all-gather.8.cloned.1.call-start = ((), (), s32[]{:S(2)}) async-start(), calls=%async_computation.4 | async-start | bytes 1966080 | tf_op jit(solution)/shard_map/all_gather | solution.py:107
  253.7 72.6 %copy-start.10 = (f32[128,512]{1,0:T(8,128)S(1)}, f32[128,512]{1,0:T(8,128)}, u32[]{:S(2)}) copy-start(f32[128,512]{1,0:T(8,128)} %param.28) | copy-start | bytes 786436
  255.8 80.1 %copy-start.11 = (f32[128,512]{1,0:T(8,128)S(1)}, f32[128,512]{1,0:T(8,128)}, u32[]{:S(2)}) copy-start(f32[128,512]{1,0:T(8,128)} %param.29) | copy-start | bytes 786436
  327.3 21.8 %copy-start.7 = (f32[128,512]{1,0:T(8,128)}, f32[128,512]{1,0:T(8,128)S(1)}, u32[]{:S(2)}) copy-start(f32[128,512]{1,0:T(8,128)S(1)} %sub.18) | copy-start | bytes 786436
  328.7 22.4 %copy-start.8 = (bf16[128,512]{1,0:T(8,128)(2,1)}, bf16[128,512]{1,0:T(8,128)(2,1)S(1)}, u32[]{:S(2)}) copy-start(bf16[128,512]{1,0:T(8,128)(2,1)S(1)} %fusion.6) | copy-start | bytes 393220
Sparse Core Ops, SparseCore 0:
  44.9 100.8 all-gather.3
  184.2 36.0 reduce-scatter.1
  223.7 19.6 all-gather.5
  250.6 75.6 all-reduce.2
  327.7 18.7 all-gather.7
